TPU v7x, 256 devices: a whole 4x4x8 slice. The times are simulated.
256 devices in a mesh: src: 16 (over x, z_lo), rcv: 16 (over z_hi, y, core).
Axes of the slice: x: 4, y: 4, z: 8 (z_hi: 2, z_lo: 4; z = z_hi * 4 + z_lo), core: 2. Of those that a mesh axis runs over, the one named last changes fastest.
Arguments:
- reflection: bfloat16 [2, 8, 16384, 4096], P(None, None, 'src', 'rcv'), may hold values from -0.25 to 0.25
- focusing: bfloat16 [96, 4096, 128], P('src', 'rcv'), may hold values from -6 to 6
- direct: bfloat16 [96, 4096, 128], P('src', 'rcv'), may hold values from -6 to 6
- onset_source: int32 [96, 16384], P(None, 'src'), may hold values from 32 to 128
- onset_receiver: int32 [96, 4096], P('src', 'rcv'), may hold values from 32 to 128
Outputs:
- upgoing: bfloat16 [96, 16384, 128], P('rcv', 'src')
- refocused: float32 [96, 4096, 128], P('src', 'rcv')
All inputs are finite; a program needn't handle non-finite values.
Results may differ from a plain program's by a relative error of at most 0.022.
Values may be sent and summed in bfloat16 or wider, within the bound.
No kernel may reach another device: no remote copies, remote signals or barrier semaphores. Data moves between devices by JAX's collectives and lax.ppermute only.
A program may use at most 192 MiB of HBM per device.

v0:
```python
import math

import jax
import jax.numpy as jnp
from jax import lax
from jax.sharding import PartitionSpec as P

NF = 8
NT = 128
NV = 96


def tables():
    steps_t = jnp.arange(NT, dtype=jnp.int32)
    bins = jnp.arange(1, NF + 1, dtype=jnp.int32)
    phase = 2.0 * math.pi / NT * (bins[:, None] * steps_t[None, :] % NT).astype(jnp.float32)
    return (jnp.cos(phase), jnp.sin(phase))


def to_spectra(field, cosines, sines):
    real_part = jnp.einsum("kt,vxt->kxv", cosines, field, precision=lax.Precision.HIGHEST)
    imaginary_component = -jnp.einsum("kt,vxt->kxv", sines, field, precision=lax.Precision.HIGHEST)
    return jnp.stack([real_part, imaginary_component]).astype(jnp.bfloat16)


def to_samples(real_part, imaginary_component, cosines, sines):
    first = jnp.einsum("kxv,kt->vxt", real_part, cosines, precision=lax.Precision.HIGHEST)
    second = jnp.einsum("kxv,kt->vxt", imaginary_component, sines, precision=lax.Precision.HIGHEST)
    return 2.0 / NT * (first - second)


def time_window(field, onsets):
    steps_t = jnp.arange(NT, dtype=jnp.int32)
    keep = steps_t[None, None, :] < onsets[:, :, None]
    return jnp.where(keep, field, jnp.zeros_like(field))


def product(left_operand, right_operand):
    return jnp.einsum(
        "pon,pna->poa", left_operand, right_operand, preferred_element_type=jnp.float32
    )


def adjoint_operator(left_operand, right_operand):
    return jnp.einsum(
        "yat,yai->iyt", left_operand, right_operand, preferred_element_type=jnp.float32
    )


def on_device(reflection, focusing, direct, onset_source, onset_receiver):
    cosines, sines = tables()
    resp_re = reflection[0]
    resp_im = reflection[1]
    gathered = lax.all_gather(focusing, "src", axis=0, tiled=True)
    spectra = to_spectra(gathered.astype(jnp.float32), cosines, sines)
    partial_value = jnp.stack(
        [
            product(resp_re, spectra[0]) - product(resp_im, spectra[1]),
            product(resp_re, spectra[1]) + product(resp_im, spectra[0]),
        ]
    )
    points_rcv = NV // lax.axis_size("rcv")
    first_point = lax.axis_index("rcv") * points_rcv
    share = lax.psum_scatter(
        partial_value.astype(jnp.bfloat16), "rcv", scatter_dimension=3, tiled=True
    ).astype(jnp.float32)
    onsets = lax.dynamic_slice_in_dim(onset_source, first_point, points_rcv, 0)
    upgoing = time_window(to_samples(share[0], share[1], cosines, sines), onsets).astype(
        jnp.bfloat16
    )
    wave = to_spectra(upgoing.astype(jnp.float32), cosines, sines)
    waves = lax.all_gather(wave, "rcv", axis=3, tiled=True)
    wave_re = waves[0]
    wave_im = waves[1]
    back_re = adjoint_operator(resp_re, wave_re) + adjoint_operator(resp_im, wave_im)
    back_im = adjoint_operator(resp_re, wave_im) - adjoint_operator(resp_im, wave_re)
    share_back = lax.psum_scatter(
        jnp.stack([back_re, back_im], axis=1).astype(jnp.bfloat16),
        "src",
        scatter_dimension=0,
        tiled=True,
    ).astype(jnp.float32)
    first = jnp.einsum("vkx,kt->vxt", share_back[:, 0], cosines, precision=lax.Precision.HIGHEST)
    second = jnp.einsum("vkx,kt->vxt", share_back[:, 1], sines, precision=lax.Precision.HIGHEST)
    downward = 2.0 / NT * (first - second)
    refocused = direct.astype(jnp.float32) + time_window(downward, onset_receiver)
    return (upgoing, refocused)


def solution(mesh):
    in_specs = (
        P(None, None, "src", "rcv"),
        P("src", "rcv", None),
        P("src", "rcv", None),
        P(None, "src"),
        P("src", "rcv"),
    )
    out_specs = (P("rcv", "src", None), P("src", "rcv", None))
    return jax.shard_map(
        on_device, mesh=mesh, in_specs=in_specs, out_specs=out_specs, check_vma=False
    )
```

profile of v0, /device:TPU:8, one launch (start us, length us, event | category | flops | bytes accessed | tf_op | source)
XLA Modules:
  0.0 453.0 jit_solution(16208150100017662029)
XLA Ops:
  7.2 0.0 all-gather.3.cloned.1.call-start
  7.2 0.7 all-gather.3.cloned.1.call-update
  7.9 0.0 reduce-scatter.3.cloned.1.call-start
  8.0 148.5 %all-gather.3.cloned.1.call-done = bf16[96,256,128]{2,1,0:T(8,128)(2,1)} async-done(((bf16[6,256,128]{2,1,0:T(8,128)(2,1)}), bf16[96,256,128]{2,1,0:T(8,128)(2,1)}) %all-gather.3.cloned.1.call-update) | async-done | bytes 6291472 | tf_op jit(solution)/shard_map/all_gather | solution.py:54
  156.5 8.0 %convolution_convert_fusion = bf16[8,96,256]{2,0,1:T(8,128)(2,1)S(1)} fusion(bf16[96,256,128]{2,1,0:T(8,128)(2,1)} %all-gather.3.cloned.1.call-done, s32[8]{0:T(128)S(1)} %iota_add_fusion), kind=kOutput, calls=%fused_computation.48 | convolution fusion | flops 302200832 | bytes 6684704 | tf_op jit(solution)/shard_map/kt,vxt->kxv/dot_general | solution.py:21
  164.4 3.7 fusion.4
  168.2 5.1 %fusion.62 = bf16[8,96,256]{2,0,1:T(8,128)(2,1)S(1)} fusion(bf16[96,256,128]{2,1,0:T(8,128)(2,1)S(1)} %copy-done.1, s32[8]{0:T(128)S(1)} %iota_add_fusion), kind=kOutput, calls=%fused_computation.47 | convolution fusion | flops 302397440 | bytes 6684704 | tf_op jit(solution)/shard_map/kt,vxt->kxv/dot_general | solution.py:22
  173.3 1.4 fusion.6
  174.7 1.4 fusion.32
  176.1 1.4 fusion.29
  177.5 0.3 pad_maximum_fusion
  177.8 3.4 copy.26
  181.2 0.2 all-gather.5.cloned.1.call-start
  181.5 92.7 %reduce-scatter.3.cloned.1.call-done = bf16[2,8,1024,6]{2,1,0,3:T(8,128)(2,1)} async-done(((bf16[2,8,1024,96]{2,1,0,3:T(8,128)(2,1)}), bf16[2,8,1024,6]{2,1,0,3:T(8,128)(2,1)}) %reduce-scatter.3.cloned.1.call-update) | async-done | bytes 196624 | tf_op jit(solution)/shard_map/reduce_scatter | solution.py:64
  274.2 2.5 fusion.80
  276.7 2.0 fusion.16
  278.7 0.9 fusion.75
  279.7 0.9 fusion.74
  280.6 0.7 pad_maximum_fusion.2
  281.3 0.0 reduce-scatter.5.cloned.1.call-start
  281.4 66.5 %all-gather.5.cloned.1.call-done = bf16[2,8,1024,96]{2,1,3,0:T(8,128)(2,1)} async-done(((bf16[2,8,1024,6]{2,1,3,0:T(8,128)(2,1)}), bf16[2,8,1024,96]{2,1,3,0:T(8,128)(2,1)}) %all-gather.5.cloned.1.call-update) | async-done | bytes 3145744 | tf_op jit(solution)/shard_map/all_gather | solution.py:72
  347.8 2.2 slice_bitcast_fusion
  350.0 3.5 fusion.2
  353.6 3.5 fusion
  357.1 1.2 fusion.63
  358.3 1.2 fusion.68
  359.5 0.1 pad_maximum_fusion.1
  359.6 1.3 copy.35
  361.0 1.6 copy.38
  362.6 80.2 %reduce-scatter.5.cloned.1.call-done = bf16[6,2,8,256]{3,2,1,0:T(8,128)(2,1)} async-done(((bf16[96,2,8,256]{3,2,1,0:T(8,128)(2,1)}), bf16[6,2,8,256]{3,2,1,0:T(8,128)(2,1)}) %reduce-scatter.5.cloned.1.call-update) | async-done | bytes 49168 | tf_op jit(solution)/shard_map/reduce_scatter | solution.py:77
  442.8 1.3 fusion.81
  444.1 2.3 fusion.41
  (25 shorter events, 0.1 us)
Async XLA Ops:
  7.2 174.3 %copy-start = (s32[96,1024]{1,0:T(8,128)S(1)}, s32[96,1024]{1,0:T(8,128)}, u32[]{:S(2)}) copy-start(s32[96,1024]{1,0:T(8,128)} %param.8) | copy-start | bytes 1179652
  7.2 149.3 %all-gather.3.cloned.1.call-start = ((), (), s32[]{:S(2)}) async-start(), calls=%async_computation.2 | async-start | bytes 6684672 | tf_op jit(solution)/shard_map/all_gather | solution.py:54
  7.9 266.3 %reduce-scatter.3.cloned.1.call-start = ((), (), s32[]{:S(2)}) async-start(), calls=%async_computation.3 | async-start | bytes 3342336 | tf_op jit(solution)/shard_map/reduce_scatter | solution.py:64
  156.5 11.7 %copy-start.1 = (bf16[96,256,128]{2,1,0:T(8,128)(2,1)S(1)}, bf16[96,256,128]{2,1,0:T(8,128)(2,1)}, u32[]{:S(2)}) copy-start(bf16[96,256,128]{2,1,0:T(8,128)(2,1)} %all-gather.3.cloned.1.call-done) | copy-start | bytes 18874372
  156.5 16.8 %slice-start = ((s8[8388608]{0:T(1024)(128)(4,1)}), s8[4194304]{0:T(1024)(128)(4,1)S(1)}, s32[]{:S(2)}) async-start(s8[8388608]{0:T(1024)(128)(4,1)} %bitcast.112), calls=%async_computation.6 | async-start | bytes 8388608
  164.4 8.8 %slice-start.1 = ((s8[8388608]{0:T(1024)(128)(4,1)}), s8[4194304]{0:T(1024)(128)(4,1)S(1)}, s32[]{:S(2)}) async-start(s8[8388608]{0:T(1024)(128)(4,1)} %bitcast.112), calls=%async_computation.7 | async-start | bytes 8388608
  181.2 166.6 %all-gather.5.cloned.1.call-start = ((), (), s32[]{:S(2)}) async-start(), calls=%async_computation.4 | async-start | bytes 3342336 | tf_op jit(solution)/shard_map/all_gather | solution.py:72
  274.2 2.5 copy-start.3
  281.3 161.5 %reduce-scatter.5.cloned.1.call-start = ((), (), s32[]{:S(2)}) async-start(), calls=%async_computation.5 | async-start | bytes 835584 | tf_op jit(solution)/shard_map/reduce_scatter | solution.py:77
  350.0 7.1 %slice-start.2 = ((s8[8388608]{0:T(1024)(128)(4,1)}), s8[4194304]{0:T(1024)(128)(4,1)S(1)}, s32[]{:S(2)}) async-start(s8[8388608]{0:T(1024)(128)(4,1)} %bitcast.114), calls=%async_computation.8 | async-start | bytes 8388608
  353.6 3.6 slice-start.3
  359.6 84.5 %copy-start.2 = (bf16[6,256,128]{2,1,0:T(8,128)(2,1)S(1)}, bf16[6,256,128]{2,1,0:T(8,128)(2,1)}, u32[]{:S(2)}) copy-start(bf16[6,256,128]{2,1,0:T(8,128)(2,1)} %param.7) | copy-start | bytes 1179652
  359.6 84.5 %copy-start.4 = (s32[6,256]{1,0:T(8,128)S(1)}, s32[6,256]{1,0:T(8,128)}, u32[]{:S(2)}) copy-start(s32[6,256]{1,0:T(8,128)} %param.9) | copy-start | bytes 18436
Sparse Core Ops, SparseCore 0:
  9.8 146.6 all-gather.2
  181.4 92.7 reduce-scatter.2
  281.4 66.3 all-gather.4
  361.1 81.6 reduce-scatter.4
where the time goes:
time: 453 us
  waiting for transfers between devices  389 us (86%)
  matrix products  40.5 us (9%)
  between operations  14 us (3%)
  local copies, waits for them, and re-layouts  8.52 us (2%)
    all_gather x1, waiting for transfers between devices, on_device(): gathered = lax.all_gather(focusing, 'src', axis=0, tiled=True)  148 us
    reduce_scatter x1, waiting for transfers between devices, on_device(): lax.psum_scatter(partial_value.astype(jnp.bfloat16), 'rcv', scatter_dimen...  92.7 us
    reduce_scatter x1, waiting for transfers between devices, on_device(): lax.psum_scatter(jnp.stack([back_re, back_im], axis=1).astype(jnp.bfloat1...  80.2 us
    all_gather x1, waiting for transfers between devices, on_device(): waves = lax.all_gather(wave, 'rcv', axis=3, tiled=True)  66.5 us
    dot_general x4, matrix products, adjoint_operator(): jnp.einsum('yat,yai->iyt', left_operand, right_operand, preferred_element...  9.49 us
  transfers between devices with their start and end apart: 4, of which 4 were waited for; matrix products, arithmetic and copies ran while one was open for 0% of the time, Pallas kernels for 0%

commit v1 on v0

v1 whole, which is shorter than its diff:
```python
import functools
import math

import jax
import jax.numpy as jnp
import numpy as np
from jax import lax
from jax.experimental import pallas as pl
from jax.experimental.pallas import tpu as pltpu
from jax.sharding import PartitionSpec as P

NF = 8
NT = 128
NP = 6
ROWS = 2 * NF * NP
NS = 1024
NR = 256
BF = jnp.bfloat16
F32 = jnp.float32
WINDOWS = ((0, 16), (0, 32), (16, 32), (32, 16))


def split(table):
    high = table.astype(BF)
    low = (table - high.astype(np.float32)).astype(BF)
    return high, low


def tables():
    k = np.arange(1, NF + 1)[:, None]
    t = np.arange(NT)[None, :]
    phase = 2.0 * math.pi / NT * ((k * t) % NT)
    return np.cos(phase).astype(np.float32), np.sin(phase).astype(np.float32)


def spectra_table():
    cosines, sines = tables()
    full = np.zeros((NP, NF, NP, 2, NT), np.float32)
    for j in range(NP):
        full[j, :, j, 0] = cosines
        full[j, :, j, 1] = -sines
    return np.concatenate(split(full.reshape(NP, ROWS, NT)), axis=1)


def samples_table():
    cosines, sines = tables()
    full = np.zeros((NP, NT, NF, NP, 2), np.float32)
    for j in range(NP):
        full[j, :, :, j, 0] = 2.0 / NT * cosines.T
        full[j, :, :, j, 1] = -2.0 / NT * sines.T
    high, low = split(full.reshape(NP, NT, ROWS))
    return np.concatenate([high, high, low], axis=2)


def dot(a, b, ca=1, cb=0):
    return lax.dot_general(a, b, (((ca,), (cb,)), ((), ())), preferred_element_type=F32)


def hi_lo_hi(x, axis):
    high = x.astype(BF)
    low = (x - high.astype(F32)).astype(BF)
    return jnp.concatenate([high, low, high], axis=axis)


def place():
    src = lax.axis_index("src")
    rcv = lax.axis_index("rcv")
    return src // 4, src % 4, rcv // 8, (rcv // 2) % 4, rcv % 2


def call(kernel, out, name, **kw):
    params = kw.pop("params", {})
    return pl.pallas_call(
        kernel,
        out_shape=out,
        name=name,
        compiler_params=pltpu.CompilerParams(vmem_limit_bytes=48 << 20, **params),
        **kw,
    )


def spectra_kernel(f_ref, t_ref, o_ref):
    acc = jnp.zeros((2 * ROWS, NR), F32)
    for j in range(NP):
        acc += dot(t_ref[j], f_ref[j], 1, 1)
    o_ref[...] = (acc[:ROWS] + acc[ROWS:]).astype(BF)


def swap_rows(x):
    even = lax.broadcasted_iota(jnp.int32, x.shape, 0) % 2 == 0
    n = x.shape[0]
    return jnp.where(even, -pltpu.roll(x, n - 1, 0), pltpu.roll(x, 1, 0))


def conv_kernel(other, f0, f1, f2, f3, r_ref, o_ref, l1, l2):
    @pl.when((pl.program_id(0) == 0) & (pl.program_id(1) == 0))
    def _():
        x, zl, zh, y, c = place()
        core = lax.rem(c + other, 2)
        par = lax.rem(zl + core, 2)
        for dx, ref in enumerate((f0, f1, f2, f3)):
            for h in range(2):
                dz = 2 * h + par
                xb = lax.rem(x + 4 - dx, 4)
                zb = lax.rem(zl + 4 - dz, 4)
                zhb = xb // 2
                yb = lax.rem(xb, 2) * 2 + zb // 2
                to = lax.rem(yb + 4 - y, 4) * 2 + lax.rem(zhb + zh, 2)
                rows = ref[dz].astype(F32)
                swapped = swap_rows(rows)
                for k in range(NF):
                    lo = 24 * (k // 2) + 8 * (k % 2)
                    l1[k, to] = rows[lo : lo + 16].astype(BF)
                    l2[k, to] = swapped[lo : lo + 16].astype(BF)

    pair = pl.program_id(0)
    u = []
    for i in range(2):
        k = 2 * pair + i
        a1 = l1[k].reshape(128, NR)
        a2 = l2[k].reshape(128, NR)
        v = dot(a1, r_ref[0, i], 1, 1) + dot(a2, r_ref[1, i], 1, 1)
        u.append(v.reshape(8, 16, v.shape[-1]))
    first = lax.broadcasted_iota(jnp.int32, (8, 8, u[0].shape[-1]), 1) < 4
    mixed = jnp.where(first, u[0][:, 8:16], u[1][:, 0:8])
    o_ref[:, 0] = jnp.concatenate([u[0][:, 0:8], mixed, u[1][:, 8:16]], axis=1).astype(BF)


def convolve(pieces, reflection, other):
    sb = 512
    out = call(
        functools.partial(conv_kernel, other),
        jax.ShapeDtypeStruct((8, 4, 24, NS), BF),
        "conv_send" if other else "conv_keep",
        grid=(4, NS // sb),
        in_specs=[pl.BlockSpec((4, ROWS, NR), lambda p, s: (0, 0, 0))] * 4
        + [pl.BlockSpec((2, 2, sb, NR), lambda p, s: (0, p, s, 0))],
        out_specs=pl.BlockSpec((8, 1, 24, sb), lambda p, s: (0, p, 0, s)),
        scratch_shapes=[pltpu.VMEM((NF, 8, 16, NR), BF)] * 2,
        cost_estimate=pl.CostEstimate(flops=1 << 30, bytes_accessed=10 << 20, transcendentals=0),
    )(*pieces, reflection)
    return out.reshape(4, 2, ROWS, NS)


def window_kernel(k_ref, r_ref, on_ref, a_ref, t_ref, w_ref, up_ref):
    u = hi_lo_hi(k_ref[...] + r_ref[...].astype(F32), 0)
    steps = lax.broadcasted_iota(jnp.int32, (NT, NS), 0)
    acc = jnp.zeros((2 * ROWS, NS), F32)
    for j in range(NP):
        field = dot(a_ref[j], u)
        field = jnp.where(steps < on_ref[j : j + 1, :], field, 0.0).astype(BF)
        up_ref[j] = field
        acc += dot(t_ref[j], field)
    w_ref[...] = (acc[:ROWS] + acc[ROWS:]).astype(BF)


def corr_kernel(other, w0, w1, w2, w3, r_ref, o_ref, acc):
    s = pl.program_id(1)

    @pl.when(s == 0)
    def _():
        acc[...] = jnp.zeros_like(acc)

    at = 0
    for i, (lo, n) in enumerate(WINDOWS):
        m = jnp.concatenate([w[e, 0, lo : lo + n] for w in (w0, w1, w2, w3) for e in range(2)], axis=0)
        for part in range(2):
            acc[part, at : at + 8 * n] += dot(m, r_ref[part, i])
        at += 8 * n

    @pl.when(s == pl.num_programs(1) - 1)
    def _():
        x, zl, zh, y, c = place()
        even = lax.broadcasted_iota(jnp.int32, (768, NR), 0) % 2 == 0
        q = acc[1]
        g = acc[0] + jnp.where(even, pltpu.roll(q, 767, 0), -pltpu.roll(q, 1, 0))
        first = lax.broadcasted_iota(jnp.int32, (8, NR), 0) < 4
        for d in range(4):
            yb = lax.rem(y + 4 - d, 4)
            for e in range(2):
                zhb = lax.rem(zh + e, 2)
                xb = zhb * 2 + yb // 2
                b = 2 * d + e
                g0 = g[16 * b : 16 * b + 16]
                g1 = g[128 + 32 * b : 128 + 32 * b + 32]
                g2 = g[384 + 32 * b : 384 + 32 * b + 32]
                g3 = g[640 + 16 * b : 640 + 16 * b + 16]
                rows = jnp.concatenate(
                    [
                        g0[0:8],
                        jnp.where(first, g0[8:16], g1[8:16]),
                        g1[16:24],
                        g2[8:16],
                        jnp.where(first, g2[16:24], g3[0:8]),
                        g3[8:16],
                    ],
                    axis=0,
                )
                o_ref[lax.rem(xb + 4 - x, 4), lax.rem(yb, 2), 0] = rows.astype(BF)


def correlate(waves, reflection, other):
    sb = 512
    return call(
        functools.partial(corr_kernel, other),
        jax.ShapeDtypeStruct((4, 2, 2, 48, NR), BF),
        "corr_other" if other else "corr_own",
        grid=(2, NS // sb),
        in_specs=[pl.BlockSpec((2, 1, 48, sb), lambda q, s: (0, q, 0, s))] * 4
        + [pl.BlockSpec((2, 4, sb, NR), lambda q, s: (0, q, s, 0))],
        out_specs=pl.BlockSpec((4, 2, 1, 48, NR), lambda q, s: (0, 0, q, 0, 0)),
        scratch_shapes=[pltpu.VMEM((2, 768, NR), F32)],
        cost_estimate=pl.CostEstimate(flops=1 << 30, bytes_accessed=10 << 20, transcendentals=0),
    )(*[w.reshape(2, 2, 48, NS) for w in waves], reflection).reshape(4, 2, ROWS, NR)


def refocus_kernel(g0, g1, g2, g3, d_ref, on_ref, a_ref, o_ref):
    g = (g0[...].astype(F32) + g1[...].astype(F32)) + (g2[...].astype(F32) + g3[...].astype(F32))
    gt = hi_lo_hi(g.T, 1)
    steps = lax.broadcasted_iota(jnp.int32, (NR, NT), 1)
    for j in range(NP):
        field = dot(gt, a_ref[j], 1, 1)
        field = jnp.where(steps < on_ref[:, j : j + 1], field, 0.0)
        o_ref[j] = d_ref[j].astype(F32) + field


def send(value, axis, to):
    return lax.ppermute(value, axis, [(i, to(i)) for i in range(16)])


def to_x(d):
    return lambda i: (i // 4 + d) % 4 * 4 + i % 4


def to_zl(d):
    return lambda i: i // 4 * 4 + (i % 4 + d) % 4


def to_y(d):
    return lambda i: i // 8 * 8 + (i // 2 % 4 + d) % 4 * 2 + i % 2


def to_zh(i):
    return (i + 8) % 16


def to_core(i):
    return i ^ 1


def on_device(reflection, focusing, direct, onset_source, onset_receiver):
    x, zl, zh, y, c = place()
    t_spec = jnp.asarray(spectra_table())
    t_samp = jnp.asarray(samples_table())
    vm = pl.BlockSpec(memory_space=pltpu.VMEM)

    spectra = call(spectra_kernel, jax.ShapeDtypeStruct((ROWS, NR), BF), "spectra")(focusing, t_spec)
    stack = jnp.stack([spectra] + [send(spectra, "src", to_zl(d)) for d in (1, 2, 3)])
    pieces = [stack] + [send(stack, "src", to_x(d)) for d in (1, 2, 3)]

    onsets = lax.dynamic_slice_in_dim(onset_source, lax.axis_index("rcv") * NP, NP, 0)
    give = convolve(pieces, reflection, 1)
    got = send(give, "rcv", to_core)
    keep = convolve(pieces, reflection, 0)
    both = [(keep[d].astype(F32) + got[d].astype(F32)).astype(BF) for d in range(4)]
    for d in (1, 2, 3):
        both[d] = send(both[d], "rcv", to_y(d))
    total = (both[0].astype(F32) + both[1].astype(F32)) + (both[2].astype(F32) + both[3].astype(F32))
    half = send(total[1].astype(BF), "rcv", to_zh)
    wave, field = call(
        window_kernel,
        (jax.ShapeDtypeStruct((ROWS, NS), BF), jax.ShapeDtypeStruct((NP, NT, NS), BF)),
        "window",
    )(total[0], half, onsets, t_samp, t_spec)
    upgoing = field.transpose(0, 2, 1)

    pair = jnp.stack([wave, send(wave, "rcv", to_zh)])
    own = [pair] + [send(pair, "rcv", to_y(d)) for d in (1, 2, 3)]
    others = [send(w, "rcv", to_core) for w in own]
    g_own = correlate(own, reflection, 0)
    g_other = correlate(others, reflection, 1)
    halves = [jnp.where(c == 0, g_own, g_other), jnp.where(c == 0, g_other, g_own)]
    back = jnp.stack(halves, axis=2).reshape(4, 4, ROWS, NR)
    parts = [back[0]] + [send(back[d], "src", to_x(d)) for d in (1, 2, 3)]
    summed = ((parts[0].astype(F32) + parts[1].astype(F32)) + (parts[2].astype(F32) + parts[3].astype(F32))).astype(BF)
    last = [
        lax.dynamic_index_in_dim(summed, (zl + d) % 4, 0, keepdims=False) for d in range(4)
    ]
    last = [last[0]] + [send(last[d], "src", to_zl(d)) for d in (1, 2, 3)]
    refocused = call(refocus_kernel, jax.ShapeDtypeStruct((NP, NR, NT), F32), "refocus")(
        *last, direct, onset_receiver.T, t_samp
    )
    return (upgoing, refocused)


def solution(mesh):
    in_specs = (
        P(None, None, "src", "rcv"),
        P("src", "rcv", None),
        P("src", "rcv", None),
        P(None, "src"),
        P("src", "rcv"),
    )
    out_specs = (P("rcv", "src", None), P("src", "rcv", None))
    return jax.shard_map(
        on_device, mesh=mesh, in_specs=in_specs, out_specs=out_specs, check_vma=False
    )
```

time: 453 us -> 157 us (0.35)
  waiting for transfers between devices: 389 us -> 60.5 us
  starting transfers between devices: 0.34 us -> 50.3 us
  matrix products: 40.5 us -> 0 us
  Pallas kernels: 0 us -> 32 us
  between operations: 14 us -> 0.85 us
    all_gather x2 -> x0, waiting for transfers between devices: 215 us -> none  [the longest x1 148 us: on_device(): gathered = lax.all_gather(focusing, 'src', axis=0, tiled=True)]
    reduce_scatter x2 -> x0, waiting for transfers between devices: 173 us -> none  [the longest x1 92.7 us: on_device(): lax.psum_scatter(partial_value.astype(jnp.bfloat16), 'rcv', scatter_dimen...]
    ppermute x0 -> x25, waiting for transfers between devices: none -> 60.5 us  [send(): return lax.ppermute(value, axis, [(i, to(i)) for i in range(16)])]
    ppermute x0 -> x25, starting transfers between devices: none -> 50.3 us  [send(): return lax.ppermute(value, axis, [(i, to(i)) for i in range(16)])]
    dot_general x16 -> x0, matrix products: 40.5 us -> none  [the longest x4 9.49 us: adjoint_operator(): jnp.einsum('yat,yai->iyt', left_operand, right_operand, preferred_element...]
    pallas_call x0 -> x7, Pallas kernels: none -> 32 us  [the longest x2 15.9 us: convolve(): call(functools.partial(conv_kernel, other), jax.ShapeDtypeStruct((8, 4, 2...]
    another operation x2 -> x0, local copies, waits for them, and re-layouts: 4.7 us -> none  [the longest x1 3.38 us: on_device(): jnp.stack([product(resp_re, spectra[0]) - product(resp_im, spectra[1]), p...]
  transfers between devices with their start and end apart: 4 -> 25, of which waited for: 4 -> 17; matrix products, arithmetic and copies ran while one was open for 0% -> 3% of each run, Pallas kernels for 0% -> 9%
where the time goes in v1:
time: 157 us; the launch traced here: 155 us
  waiting for transfers between devices  60.5 us (39%)
  starting transfers between devices  50.3 us (32%)
  Pallas kernels  32 us (20%)
  local copies, waits for them, and re-layouts  6.05 us (4%)
  other arithmetic  4.94 us (3%)
    ppermute x25, waiting for transfers between devices, send(): return lax.ppermute(value, axis, [(i, to(i)) for i in range(16)])  60.5 us
    ppermute x25, starting transfers between devices, send(): return lax.ppermute(value, axis, [(i, to(i)) for i in range(16)])  50.3 us
    pallas_call x2, Pallas kernels, convolve(): call(functools.partial(conv_kernel, other), jax.ShapeDtypeStruct((8, 4, 2...  15.9 us
    pallas_call x2, Pallas kernels, correlate(): call(functools.partial(corr_kernel, other), jax.ShapeDtypeStruct((4, 2, 2...  12.2 us
    unnamed x18, local copies, waits for them, and re-layouts  3.73 us
  transfers between devices with their start and end apart: 25, of which 17 were waited for; matrix products, arithmetic and copies ran while one was open for 3% of the time, Pallas kernels for 9%

profile of v1, /device:TPU:8, one launch (start us, length us, event | category | flops | bytes accessed | tf_op | source)
XLA Modules:
  0.0 154.7 jit_solution(8601340889389325811)
XLA Ops:
  3.0 2.0 %collective-permute-start = (bf16[96,256]{1,0:T(8,128)(2,1)S(1)}, bf16[96,256]{1,0:T(8,128)(2,1)S(1)}, u32[]{:S(2)}, u32[]{:S(2)}) collective-permute-start(bf16[96,256]{1,0:T(8,128)(2,1)S(1)} %spectra.1), channel_id=1, source_target_pairs={{0,16},{16,32},{32,48},{48,0},{64,80},{80,96},{96,112},{112,64},{1... | collective-permute-start | bytes 147464 | tf_op jit(solution)/shard_map/ppermute | solution.py:228
  5.0 3.3 %collective-permute-start.1 = (bf16[96,256]{1,0:T(8,128)(2,1)S(1)}, bf16[96,256]{1,0:T(8,128)(2,1)S(1)}, u32[]{:S(2)}, u32[]{:S(2)}) collective-permute-start(bf16[96,256]{1,0:T(8,128)(2,1)S(1)} %spectra.1), channel_id=1, source_target_pairs={{0,32},{16,48},{32,0},{48,16},{64,96},{80,112},{96,64},{112,80},{1... | collective-permute-start | bytes 147464 | tf_op jit(solution)/shard_map/ppermute | solution.py:228
  10.1 1.7 %collective-permute-done.1 = bf16[96,256]{1,0:T(8,128)(2,1)S(1)} collective-permute-done((bf16[96,256]{1,0:T(8,128)(2,1)S(1)}, bf16[96,256]{1,0:T(8,128)(2,1)S(1)}, u32[]{:S(2)}, u32[]{:S(2)}) %collective-permute-start.1) | collective-permute-done | bytes 49184 | tf_op jit(solution)/shard_map/ppermute | solution.py:228
  12.4 1.6 %collective-permute-start.3 = (bf16[4,96,256]{2,1,0:T(8,128)(2,1)S(1)}, bf16[4,96,256]{2,1,0:T(8,128)(2,1)S(1)}, u32[]{:S(2)}, u32[]{:S(2)}) collective-permute-start(bf16[4,96,256]{2,1,0:T(8,128)(2,1)S(1)} %pad_maximum_fusion.3.f0), channel_id=1, source_target_pairs={{0,64},{16,80},{32,96},{48,112},{64,128},{80,144},{96,160},{112,17... | collective-permute-start | bytes 589832 | tf_op jit(solution)/shard_map/ppermute | solution.py:228
  14.0 2.7 %collective-permute-start.4 = (bf16[4,96,256]{2,1,0:T(8,128)(2,1)S(1)}, bf16[4,96,256]{2,1,0:T(8,128)(2,1)S(1)}, u32[]{:S(2)}, u32[]{:S(2)}) collective-permute-start(bf16[4,96,256]{2,1,0:T(8,128)(2,1)S(1)} %pad_maximum_fusion.3.f0), channel_id=1, source_target_pairs={{0,128},{16,144},{32,160},{48,176},{64,192},{80,208},{96,224},{112... | collective-permute-start | bytes 589832 | tf_op jit(solution)/shard_map/ppermute | solution.py:228
  18.1 2.4 %collective-permute-done.3.f1 = bf16[4,96,256]{2,1,0:T(8,128)(2,1)S(1)} collective-permute-done((bf16[4,96,256]{2,1,0:T(8,128)(2,1)S(1)}, bf16[4,96,256]{2,1,0:T(8,128)(2,1)S(1)}, u32[]{:S(2)}, u32[]{:S(2)}) %collective-permute-start.3) | collective-permute-done | bytes 196640 | tf_op jit(solution)/shard_map/ppermute | solution.py:228
  20.5 4.1 %collective-permute-done.4.f2 = bf16[4,96,256]{2,1,0:T(8,128)(2,1)S(1)} collective-permute-done((bf16[4,96,256]{2,1,0:T(8,128)(2,1)S(1)}, bf16[4,96,256]{2,1,0:T(8,128)(2,1)S(1)}, u32[]{:S(2)}, u32[]{:S(2)}) %collective-permute-start.4) | collective-permute-done | bytes 196640 | tf_op jit(solution)/shard_map/ppermute | solution.py:228
  24.6 7.9 %conv_send.1 = bf16[8,4,24,1024]{3,2,1,0:T(8,128)(2,1)S(1)} custom-call(bf16[4,96,256]{2,1,0:T(8,128)(2,1)S(1)} %pad_maximum_fusion.3.f0, bf16[4,96,256]{2,1,0:T(8,128)(2,1)S(1)} %collective-permute-done.3.f1, bf16[4,96,256]{2,1,0:T(8,128)(2,1)S(1)} %collective-permute-done.4.f2, bf16[4,96,256]{2,1,0:T(8,128)(2,1)S(1)} %collective-permute-done.5.f3, ...), custom_call_target="tpu_custom_call" | custom-call | flops 1073741824 | bytes 10485760 | tf_op jit(solution)/shard_map/conv_send/pallas_call | solution.py:131
  32.6 8.0 %conv_keep.1 = bf16[8,4,24,1024]{3,2,1,0:T(8,128)(2,1)S(1)} custom-call(bf16[4,96,256]{2,1,0:T(8,128)(2,1)S(1)} %pad_maximum_fusion.3.f0, bf16[4,96,256]{2,1,0:T(8,128)(2,1)S(1)} %collective-permute-done.3.f1, bf16[4,96,256]{2,1,0:T(8,128)(2,1)S(1)} %collective-permute-done.4.f2, bf16[4,96,256]{2,1,0:T(8,128)(2,1)S(1)} %collective-permute-done.5.f3, ...), custom_call_target="tpu_custom_call" | custom-call | flops 1073741824 | bytes 10485760 | tf_op jit(solution)/shard_map/conv_keep/pallas_call | solution.py:131
  42.1 1.6 %collective-permute-start.7 = (bf16[2,96,1024]{2,1,0:T(8,128)(2,1)}, bf16[2,96,1024]{2,1,0:T(8,128)(2,1)}, u32[]{:S(2)}, u32[]{:S(2)}) collective-permute-start(bf16[2,96,1024]{2,1,0:T(8,128)(2,1)} %get-tuple-element.12), channel_id=1, source_target_pairs={{0,2},{1,3},{2,4},{3,5},{4,6},{5,7},{6,0},{7,1},{8,10},{9,11},{10,... | collective-permute-start | bytes 1179656 | tf_op jit(solution)/shard_map/ppermute | solution.py:228
  44.6 2.4 %collective-permute-start.9 = (bf16[2,96,1024]{2,1,0:T(8,128)(2,1)S(1)}, bf16[2,96,1024]{2,1,0:T(8,128)(2,1)}, u32[]{:S(2)}, u32[]{:S(2)}) collective-permute-start(bf16[2,96,1024]{2,1,0:T(8,128)(2,1)S(1)} %get-tuple-element.13), channel_id=1, source_target_pairs={{0,6},{1,7},{2,0},{3,1},{4,2},{5,3},{6,4},{7,5},{8,14},{9,15},{10,... | collective-permute-start | bytes 1179656 | tf_op jit(solution)/shard_map/ppermute | solution.py:228
  47.0 7.3 %collective-permute-done.7 = bf16[2,96,1024]{2,1,0:T(8,128)(2,1)} collective-permute-done((bf16[2,96,1024]{2,1,0:T(8,128)(2,1)}, bf16[2,96,1024]{2,1,0:T(8,128)(2,1)}, u32[]{:S(2)}, u32[]{:S(2)}) %collective-permute-start.7) | collective-permute-done | bytes 393248 | tf_op jit(solution)/shard_map/ppermute | solution.py:228
  54.3 3.0 %collective-permute-done.8 = bf16[2,96,1024]{2,1,0:T(8,128)(2,1)} collective-permute-done((bf16[2,96,1024]{2,1,0:T(8,128)(2,1)S(1)}, bf16[2,96,1024]{2,1,0:T(8,128)(2,1)}, u32[]{:S(2)}, u32[]{:S(2)}) %collective-permute-start.8) | collective-permute-done | bytes 393248 | tf_op jit(solution)/shard_map/ppermute | solution.py:228
  57.3 6.8 %collective-permute-done.9 = bf16[2,96,1024]{2,1,0:T(8,128)(2,1)} collective-permute-done((bf16[2,96,1024]{2,1,0:T(8,128)(2,1)S(1)}, bf16[2,96,1024]{2,1,0:T(8,128)(2,1)}, u32[]{:S(2)}, u32[]{:S(2)}) %collective-permute-start.9) | collective-permute-done | bytes 393248 | tf_op jit(solution)/shard_map/ppermute | solution.py:228
  64.1 1.6 %add_add_fusion = f32[2,96,1024]{2,1,0:T(8,128)S(1)} fusion(bf16[2,96,1024]{2,1,0:T(8,128)(2,1)} %collective-permute-done.9, bf16[2,96,1024]{2,1,0:T(8,128)(2,1)} %collective-permute-done.8, bf16[2,96,1024]{2,1,0:T(8,128)(2,1)} %collective-permute-done.7, bf16[4,2,96,1024]{3,2,1,0:T(8,128)(2,1)S(1)} %collective-permute-done.6, ...), kind=kLoop, calls=%fused_computation.14 | loop fusion | flops 2162688 | bytes 2752512 | tf_op jit(solution)/shard_map/add | solution.py:268
  65.8 6.1 %collective-permute-start.10 = (bf16[96,1024]{1,0:T(8,128)(2,1)S(1)}, bf16[96,1024]{1,0:T(8,128)(2,1)S(1)}, u32[]{:S(2)}, u32[]{:S(2)}) collective-permute-start(bf16[96,1024]{1,0:T(8,128)(2,1)S(1)} %fusion.6), channel_id=1, source_target_pairs={{0,8},{1,9},{2,10},{3,11},{4,12},{5,13},{6,14},{7,15},{8,0},{9,1},... | collective-permute-start | bytes 589832 | tf_op jit(solution)/shard_map/ppermute | solution.py:228
  71.9 6.2 %collective-permute-done.10.r_ref = bf16[96,1024]{1,0:T(8,128)(2,1)S(1)} collective-permute-done((bf16[96,1024]{1,0:T(8,128)(2,1)S(1)}, bf16[96,1024]{1,0:T(8,128)(2,1)S(1)}, u32[]{:S(2)}, u32[]{:S(2)}) %collective-permute-start.10) | collective-permute-done | bytes 196640 | tf_op jit(solution)/shard_map/ppermute | solution.py:228
  78.2 2.1 %window.1 = (bf16[96,1024]{1,0:T(8,128)(2,1)S(1)}, bf16[6,128,1024]{2,1,0:T(8,128)(2,1)S(1)}) custom-call(f32[96,1024]{1,0:T(8,128)S(1)} %slice_bitcast_fusion.k_ref, bf16[96,1024]{1,0:T(8,128)(2,1)S(1)} %collective-permute-done.10.r_ref, s32[6,1024]{1,0:T(8,128)S(1)} %constant_dynamic-slice_fusion.on_ref, bf16[6,128,288]{2,1,0:T(8,128)(2,1)S(1)} %copy-done.1, ...), custom_call_target="tpu_custom_call" | custom-call | tf_op jit(solution)/shard_map/window/pallas_call | solution.py:270
  80.3 6.2 %collective-permute-start.11 = (bf16[96,1024]{1,0:T(8,128)(2,1)S(1)}, bf16[96,1024]{1,0:T(8,128)(2,1)S(1)}, u32[]{:S(2)}, u32[]{:S(2)}) collective-permute-start(bf16[96,1024]{1,0:T(8,128)(2,1)S(1)} %get-tuple-element.5), channel_id=1, source_target_pairs={{0,8},{1,9},{2,10},{3,11},{4,12},{5,13},{6,14},{7,15},{8,0},{9,1},... | collective-permute-start | bytes 589832 | tf_op jit(solution)/shard_map/ppermute | solution.py:228
  86.4 5.3 %collective-permute-done.11 = bf16[96,1024]{1,0:T(8,128)(2,1)S(1)} collective-permute-done((bf16[96,1024]{1,0:T(8,128)(2,1)S(1)}, bf16[96,1024]{1,0:T(8,128)(2,1)S(1)}, u32[]{:S(2)}, u32[]{:S(2)}) %collective-permute-start.11) | collective-permute-done | bytes 196640 | tf_op jit(solution)/shard_map/ppermute | solution.py:228
  94.1 2.2 %collective-permute-start.13 = (bf16[2,96,1024]{2,1,0:T(8,128)(2,1)}, bf16[2,96,1024]{2,1,0:T(8,128)(2,1)}, u32[]{:S(2)}, u32[]{:S(2)}) collective-permute-start(bf16[2,96,1024]{2,1,0:T(8,128)(2,1)} %pad_maximum_fusion.1), channel_id=1, source_target_pairs={{0,4},{1,5},{2,6},{3,7},{4,0},{5,1},{6,2},{7,3},{8,12},{9,13},{10,... | collective-permute-start | bytes 1179656 | tf_op jit(solution)/shard_map/ppermute | solution.py:228
  96.6 7.1 %collective-permute-done.12 = bf16[2,96,1024]{2,1,0:T(8,128)(2,1)S(1)} collective-permute-done((bf16[2,96,1024]{2,1,0:T(8,128)(2,1)}, bf16[2,96,1024]{2,1,0:T(8,128)(2,1)S(1)}, u32[]{:S(2)}, u32[]{:S(2)}) %collective-permute-start.12) | collective-permute-done | bytes 393248 | tf_op jit(solution)/shard_map/ppermute | solution.py:228
  103.7 2.4 %collective-permute-done.13 = bf16[2,96,1024]{2,1,0:T(8,128)(2,1)} collective-permute-done((bf16[2,96,1024]{2,1,0:T(8,128)(2,1)}, bf16[2,96,1024]{2,1,0:T(8,128)(2,1)}, u32[]{:S(2)}, u32[]{:S(2)}) %collective-permute-start.13) | collective-permute-done | bytes 393248 | tf_op jit(solution)/shard_map/ppermute | solution.py:228
  106.1 4.1 %collective-permute-done.14 = bf16[2,96,1024]{2,1,0:T(8,128)(2,1)} collective-permute-done((bf16[2,96,1024]{2,1,0:T(8,128)(2,1)}, bf16[2,96,1024]{2,1,0:T(8,128)(2,1)}, u32[]{:S(2)}, u32[]{:S(2)}) %collective-permute-start.14) | collective-permute-done | bytes 393248 | tf_op jit(solution)/shard_map/ppermute | solution.py:228
  111.2 6.1 %corr_own.1 = bf16[4,2,2,48,256]{4,3,2,1,0:T(8,128)(2,1)S(1)} custom-call(bf16[2,2,48,1024]{3,2,1,0:T(8,128)(2,1)S(1)} %pad_maximum_fusion.w0, bf16[2,2,48,1024]{3,2,1,0:T(8,128)(2,1)S(1)} %bitcast.79, bf16[2,2,48,1024]{3,2,1,0:T(8,128)(2,1)} %bitcast.21.w2, bf16[2,2,48,1024]{3,2,1,0:T(8,128)(2,1)} %bitcast.22.w3, bf16[2,8,1024,256]{3,2,1,0:T(8,128)(2,1)} %r_ref.7), custom_call_target="tpu_custom_call" | custom-call | flops 1073741824 | bytes 10485760 | tf_op jit(solution)/shard_map/corr_own/pallas_call | solution.py:204
  117.3 6.1 %corr_other.1 = bf16[4,2,2,48,256]{4,3,2,1,0:T(8,128)(2,1)S(1)} custom-call(bf16[2,2,48,1024]{3,2,1,0:T(8,128)(2,1)S(1)} %bitcast.78, bf16[2,2,48,1024]{3,2,1,0:T(8,128)(2,1)} %bitcast.24.w1, bf16[2,2,48,1024]{3,2,1,0:T(8,128)(2,1)} %bitcast.25.w2, bf16[2,2,48,1024]{3,2,1,0:T(8,128)(2,1)} %bitcast.26.w3, bf16[2,8,1024,256]{3,2,1,0:T(8,128)(2,1)} %r_ref.7), custom_call_target="tpu_custom_call" | custom-call | flops 1073741824 | bytes 10485760 | tf_op jit(solution)/shard_map/corr_other/pallas_call | solution.py:204
  126.1 2.4 %collective-permute-start.20 = (bf16[4,96,256]{2,1,0:T(8,128)(2,1)}, bf16[4,96,256]{2,1,0:T(8,128)(2,1)S(1)}, u32[]{:S(2)}, u32[]{:S(2)}) collective-permute-start(bf16[4,96,256]{2,1,0:T(8,128)(2,1)} %bitcast.31), channel_id=1, source_target_pairs={{0,128},{16,144},{32,160},{48,176},{64,192},{80,208},{96,224},{112... | collective-permute-start | bytes 589832 | tf_op jit(solution)/shard_map/ppermute | solution.py:228
  129.2 1.6 %collective-permute-start.21 = (bf16[4,96,256]{2,1,0:T(8,128)(2,1)}, bf16[4,96,256]{2,1,0:T(8,128)(2,1)S(1)}, u32[]{:S(2)}, u32[]{:S(2)}) collective-permute-start(bf16[4,96,256]{2,1,0:T(8,128)(2,1)} %bitcast.32), channel_id=1, source_target_pairs={{0,192},{16,208},{32,224},{48,240},{64,0},{80,16},{96,32},{112,48}... | collective-permute-start | bytes 589832 | tf_op jit(solution)/shard_map/ppermute | solution.py:228
  130.9 2.1 %collective-permute-done.19 = bf16[4,96,256]{2,1,0:T(8,128)(2,1)S(1)} collective-permute-done((bf16[4,96,256]{2,1,0:T(8,128)(2,1)}, bf16[4,96,256]{2,1,0:T(8,128)(2,1)S(1)}, u32[]{:S(2)}, u32[]{:S(2)}) %collective-permute-start.19) | collective-permute-done | bytes 196640 | tf_op jit(solution)/shard_map/ppermute | solution.py:228
  133.0 4.6 %collective-permute-done.20 = bf16[4,96,256]{2,1,0:T(8,128)(2,1)S(1)} collective-permute-done((bf16[4,96,256]{2,1,0:T(8,128)(2,1)}, bf16[4,96,256]{2,1,0:T(8,128)(2,1)S(1)}, u32[]{:S(2)}, u32[]{:S(2)}) %collective-permute-start.20) | collective-permute-done | bytes 196640 | tf_op jit(solution)/shard_map/ppermute | solution.py:228
  138.6 9.3 %collective-permute-start.22 = (bf16[96,256]{1,0:T(8,128)(2,1)S(1)}, bf16[96,256]{1,0:T(8,128)(2,1)S(1)}, u32[]{:S(2)}, u32[]{:S(2)}) collective-permute-start(bf16[96,256]{1,0:T(8,128)(2,1)S(1)} %get-tuple-element.23), channel_id=1, source_target_pairs={{0,16},{16,32},{32,48},{48,0},{64,80},{80,96},{96,112},{112,64},{1... | collective-permute-start | bytes 147464 | tf_op jit(solution)/shard_map/ppermute | solution.py:228
  147.9 2.5 %collective-permute-start.24 = (bf16[96,256]{1,0:T(8,128)(2,1)S(1)}, bf16[96,256]{1,0:T(8,128)(2,1)S(1)}, u32[]{:S(2)}, u32[]{:S(2)}) collective-permute-start(bf16[96,256]{1,0:T(8,128)(2,1)S(1)} %get-tuple-element.21), channel_id=1, source_target_pairs={{0,48},{16,0},{32,16},{48,32},{64,112},{80,64},{96,80},{112,96},{1... | collective-permute-start | bytes 147464 | tf_op jit(solution)/shard_map/ppermute | solution.py:228
  (60 shorter events, 21.0 us)
Async XLA Ops:
  0.6 46.4 %copy-start = (s32[96,1024]{1,0:T(8,128)S(1)}, s32[96,1024]{1,0:T(8,128)}, u32[]{:S(2)}) copy-start(s32[96,1024]{1,0:T(8,128)} %param.10) | copy-start | bytes 1179652
  0.6 1.0 copy-start.2
  3.0 7.1 %collective-permute-start = (bf16[96,256]{1,0:T(8,128)(2,1)S(1)}, bf16[96,256]{1,0:T(8,128)(2,1)S(1)}, u32[]{:S(2)}, u32[]{:S(2)}) collective-permute-start(bf16[96,256]{1,0:T(8,128)(2,1)S(1)} %spectra.1), channel_id=1, source_target_pairs={{0,16},{16,32},{32,48},{48,0},{64,80},{80,96},{96,112},{112,64},{1... | collective-permute-start | bytes 147464 | tf_op jit(solution)/shard_map/ppermute | solution.py:228
  5.0 6.9 %collective-permute-start.1 = (bf16[96,256]{1,0:T(8,128)(2,1)S(1)}, bf16[96,256]{1,0:T(8,128)(2,1)S(1)}, u32[]{:S(2)}, u32[]{:S(2)}) collective-permute-start(bf16[96,256]{1,0:T(8,128)(2,1)S(1)} %spectra.1), channel_id=1, source_target_pairs={{0,32},{16,48},{32,0},{48,16},{64,96},{80,112},{96,64},{112,80},{1... | collective-permute-start | bytes 147464 | tf_op jit(solution)/shard_map/ppermute | solution.py:228
  8.2 4.1 %collective-permute-start.2 = (bf16[96,256]{1,0:T(8,128)(2,1)S(1)}, bf16[96,256]{1,0:T(8,128)(2,1)S(1)}, u32[]{:S(2)}, u32[]{:S(2)}) collective-permute-start(bf16[96,256]{1,0:T(8,128)(2,1)S(1)} %spectra.1), channel_id=1, source_target_pairs={{0,48},{16,0},{32,16},{48,32},{64,112},{80,64},{96,80},{112,96},{1... | collective-permute-start | bytes 147464 | tf_op jit(solution)/shard_map/ppermute | solution.py:228
  12.4 8.1 %collective-permute-start.3 = (bf16[4,96,256]{2,1,0:T(8,128)(2,1)S(1)}, bf16[4,96,256]{2,1,0:T(8,128)(2,1)S(1)}, u32[]{:S(2)}, u32[]{:S(2)}) collective-permute-start(bf16[4,96,256]{2,1,0:T(8,128)(2,1)S(1)} %pad_maximum_fusion.3.f0), channel_id=1, source_target_pairs={{0,64},{16,80},{32,96},{48,112},{64,128},{80,144},{96,160},{112,17... | collective-permute-start | bytes 589832 | tf_op jit(solution)/shard_map/ppermute | solution.py:228
  14.0 10.6 %collective-permute-start.4 = (bf16[4,96,256]{2,1,0:T(8,128)(2,1)S(1)}, bf16[4,96,256]{2,1,0:T(8,128)(2,1)S(1)}, u32[]{:S(2)}, u32[]{:S(2)}) collective-permute-start(bf16[4,96,256]{2,1,0:T(8,128)(2,1)S(1)} %pad_maximum_fusion.3.f0), channel_id=1, source_target_pairs={{0,128},{16,144},{32,160},{48,176},{64,192},{80,208},{96,224},{112... | collective-permute-start | bytes 589832 | tf_op jit(solution)/shard_map/ppermute | solution.py:228
  16.7 7.9 %collective-permute-start.5 = (bf16[4,96,256]{2,1,0:T(8,128)(2,1)S(1)}, bf16[4,96,256]{2,1,0:T(8,128)(2,1)S(1)}, u32[]{:S(2)}, u32[]{:S(2)}) collective-permute-start(bf16[4,96,256]{2,1,0:T(8,128)(2,1)S(1)} %pad_maximum_fusion.3.f0), channel_id=1, source_target_pairs={{0,192},{16,208},{32,224},{48,240},{64,0},{80,16},{96,32},{112,48}... | collective-permute-start | bytes 589832 | tf_op jit(solution)/shard_map/ppermute | solution.py:228
  32.5 8.2 %collective-permute-start.6 = (bf16[4,2,96,1024]{3,2,1,0:T(8,128)(2,1)S(1)}, bf16[4,2,96,1024]{3,2,1,0:T(8,128)(2,1)S(1)}, u32[]{:S(2)}, u32[]{:S(2)}) collective-permute-start(bf16[4,2,96,1024]{3,2,1,0:T(8,128)(2,1)S(1)} %bitcast.74), channel_id=1, source_target_pairs={{0,1},{1,0},{2,3},{3,2},{4,5},{5,4},{6,7},{7,6},{8,9},{9,8},{10,11... | collective-permute-start | bytes 4718600 | tf_op jit(solution)/shard_map/ppermute | solution.py:228
  42.1 12.2 %collective-permute-start.7 = (bf16[2,96,1024]{2,1,0:T(8,128)(2,1)}, bf16[2,96,1024]{2,1,0:T(8,128)(2,1)}, u32[]{:S(2)}, u32[]{:S(2)}) collective-permute-start(bf16[2,96,1024]{2,1,0:T(8,128)(2,1)} %get-tuple-element.12), channel_id=1, source_target_pairs={{0,2},{1,3},{2,4},{3,5},{4,6},{5,7},{6,0},{7,1},{8,10},{9,11},{10,... | collective-permute-start | bytes 1179656 | tf_op jit(solution)/shard_map/ppermute | solution.py:228
  43.7 13.6 %collective-permute-start.8 = (bf16[2,96,1024]{2,1,0:T(8,128)(2,1)S(1)}, bf16[2,96,1024]{2,1,0:T(8,128)(2,1)}, u32[]{:S(2)}, u32[]{:S(2)}) collective-permute-start(bf16[2,96,1024]{2,1,0:T(8,128)(2,1)S(1)} %get-tuple-element.14), channel_id=1, source_target_pairs={{0,4},{1,5},{2,6},{3,7},{4,0},{5,1},{6,2},{7,3},{8,12},{9,13},{10,... | collective-permute-start | bytes 1179656 | tf_op jit(solution)/shard_map/ppermute | solution.py:228
  44.6 19.5 %collective-permute-start.9 = (bf16[2,96,1024]{2,1,0:T(8,128)(2,1)S(1)}, bf16[2,96,1024]{2,1,0:T(8,128)(2,1)}, u32[]{:S(2)}, u32[]{:S(2)}) collective-permute-start(bf16[2,96,1024]{2,1,0:T(8,128)(2,1)S(1)} %get-tuple-element.13), channel_id=1, source_target_pairs={{0,6},{1,7},{2,0},{3,1},{4,2},{5,3},{6,4},{7,5},{8,14},{9,15},{10,... | collective-permute-start | bytes 1179656 | tf_op jit(solution)/shard_map/ppermute | solution.py:228
  64.1 14.0 %copy-start.1 = (bf16[6,128,288]{2,1,0:T(8,128)(2,1)S(1)}, bf16[6,128,288]{2,1,0:T(8,128)(2,1)}, u32[]{:S(2)}) copy-start(bf16[6,128,288]{2,1,0:T(8,128)(2,1)} %constant.68.clone.a_ref) | copy-start | bytes 1327108
  64.1 14.0 %copy-start.3 = (bf16[6,192,128]{2,1,0:T(8,128)(2,1)S(1)}, bf16[6,192,128]{2,1,0:T(8,128)(2,1)}, u32[]{:S(2)}) copy-start(bf16[6,192,128]{2,1,0:T(8,128)(2,1)} %constant.67.clone.t_ref) | copy-start | bytes 884740
  65.8 12.4 %collective-permute-start.10 = (bf16[96,1024]{1,0:T(8,128)(2,1)S(1)}, bf16[96,1024]{1,0:T(8,128)(2,1)S(1)}, u32[]{:S(2)}, u32[]{:S(2)}) collective-permute-start(bf16[96,1024]{1,0:T(8,128)(2,1)S(1)} %fusion.6), channel_id=1, source_target_pairs={{0,8},{1,9},{2,10},{3,11},{4,12},{5,13},{6,14},{7,15},{8,0},{9,1},... | collective-permute-start | bytes 589832 | tf_op jit(solution)/shard_map/ppermute | solution.py:228
  80.3 11.5 %collective-permute-start.11 = (bf16[96,1024]{1,0:T(8,128)(2,1)S(1)}, bf16[96,1024]{1,0:T(8,128)(2,1)S(1)}, u32[]{:S(2)}, u32[]{:S(2)}) collective-permute-start(bf16[96,1024]{1,0:T(8,128)(2,1)S(1)} %get-tuple-element.5), channel_id=1, source_target_pairs={{0,8},{1,9},{2,10},{3,11},{4,12},{5,13},{6,14},{7,15},{8,0},{9,1},... | collective-permute-start | bytes 589832 | tf_op jit(solution)/shard_map/ppermute | solution.py:228
  91.7 4.6 %copy-start.6 = (bf16[96,1024]{1,0:T(8,128)(2,1)}, bf16[96,1024]{1,0:T(8,128)(2,1)S(1)}, u32[]{:S(2)}) copy-start(bf16[96,1024]{1,0:T(8,128)(2,1)S(1)} %collective-permute-done.11) | copy-start | bytes 589828
  92.5 11.2 %collective-permute-start.12 = (bf16[2,96,1024]{2,1,0:T(8,128)(2,1)}, bf16[2,96,1024]{2,1,0:T(8,128)(2,1)S(1)}, u32[]{:S(2)}, u32[]{:S(2)}) collective-permute-start(bf16[2,96,1024]{2,1,0:T(8,128)(2,1)} %pad_maximum_fusion.1), channel_id=1, source_target_pairs={{0,2},{1,3},{2,4},{3,5},{4,6},{5,7},{6,0},{7,1},{8,10},{9,11},{10,... | collective-permute-start | bytes 1179656 | tf_op jit(solution)/shard_map/ppermute | solution.py:228
  94.1 12.1 %collective-permute-start.13 = (bf16[2,96,1024]{2,1,0:T(8,128)(2,1)}, bf16[2,96,1024]{2,1,0:T(8,128)(2,1)}, u32[]{:S(2)}, u32[]{:S(2)}) collective-permute-start(bf16[2,96,1024]{2,1,0:T(8,128)(2,1)} %pad_maximum_fusion.1), channel_id=1, source_target_pairs={{0,4},{1,5},{2,6},{3,7},{4,0},{5,1},{6,2},{7,3},{8,12},{9,13},{10,... | collective-permute-start | bytes 1179656 | tf_op jit(solution)/shard_map/ppermute | solution.py:228
  96.3 13.9 %collective-permute-start.14 = (bf16[2,96,1024]{2,1,0:T(8,128)(2,1)}, bf16[2,96,1024]{2,1,0:T(8,128)(2,1)}, u32[]{:S(2)}, u32[]{:S(2)}) collective-permute-start(bf16[2,96,1024]{2,1,0:T(8,128)(2,1)} %pad_maximum_fusion.1), channel_id=1, source_target_pairs={{0,6},{1,7},{2,0},{3,1},{4,2},{5,3},{6,4},{7,5},{8,14},{9,15},{10,... | collective-permute-start | bytes 1179656 | tf_op jit(solution)/shard_map/ppermute | solution.py:228
  96.6 20.7 %collective-permute-start.15 = (bf16[2,96,1024]{2,1,0:T(8,128)(2,1)}, bf16[2,96,1024]{2,1,0:T(8,128)(2,1)S(1)}, u32[]{:S(2)}, u32[]{:S(2)}) collective-permute-start(bf16[2,96,1024]{2,1,0:T(8,128)(2,1)} %pad_maximum_fusion.1), channel_id=1, source_target_pairs={{0,1},{1,0},{2,3},{3,2},{4,5},{5,4},{6,7},{7,6},{8,9},{9,8},{10,11... | collective-permute-start | bytes 1179656 | tf_op jit(solution)/shard_map/ppermute | solution.py:228
  103.7 13.5 %collective-permute-start.16 = (bf16[2,96,1024]{2,1,0:T(8,128)(2,1)S(1)}, bf16[2,96,1024]{2,1,0:T(8,128)(2,1)}, u32[]{:S(2)}, u32[]{:S(2)}) collective-permute-start(bf16[2,96,1024]{2,1,0:T(8,128)(2,1)S(1)} %collective-permute-done.12), channel_id=1, source_target_pairs={{0,1},{1,0},{2,3},{3,2},{4,5},{5,4},{6,7},{7,6},{8,9},{9,8},{10,11... | collective-permute-start | bytes 1179656 | tf_op jit(solution)/shard_map/ppermute | solution.py:228
  106.1 11.1 %collective-permute-start.17 = (bf16[2,96,1024]{2,1,0:T(8,128)(2,1)}, bf16[2,96,1024]{2,1,0:T(8,128)(2,1)}, u32[]{:S(2)}, u32[]{:S(2)}) collective-permute-start(bf16[2,96,1024]{2,1,0:T(8,128)(2,1)} %collective-permute-done.13), channel_id=1, source_target_pairs={{0,1},{1,0},{2,3},{3,2},{4,5},{5,4},{6,7},{7,6},{8,9},{9,8},{10,11... | collective-permute-start | bytes 1179656 | tf_op jit(solution)/shard_map/ppermute | solution.py:228
  110.2 7.1 %collective-permute-start.18 = (bf16[2,96,1024]{2,1,0:T(8,128)(2,1)}, bf16[2,96,1024]{2,1,0:T(8,128)(2,1)}, u32[]{:S(2)}, u32[]{:S(2)}) collective-permute-start(bf16[2,96,1024]{2,1,0:T(8,128)(2,1)} %collective-permute-done.14), channel_id=1, source_target_pairs={{0,1},{1,0},{2,3},{3,2},{4,5},{5,4},{6,7},{7,6},{8,9},{9,8},{10,11... | collective-permute-start | bytes 1179656 | tf_op jit(solution)/shard_map/ppermute | solution.py:228
  124.2 8.7 %collective-permute-start.19 = (bf16[4,96,256]{2,1,0:T(8,128)(2,1)}, bf16[4,96,256]{2,1,0:T(8,128)(2,1)S(1)}, u32[]{:S(2)}, u32[]{:S(2)}) collective-permute-start(bf16[4,96,256]{2,1,0:T(8,128)(2,1)} %bitcast.30), channel_id=1, source_target_pairs={{0,64},{16,80},{32,96},{48,112},{64,128},{80,144},{96,160},{112,17... | collective-permute-start | bytes 589832 | tf_op jit(solution)/shard_map/ppermute | solution.py:228
  125.4 24.9 %copy-start.7 = (s32[6,256]{1,0:T(8,128)S(1)}, s32[6,256]{1,0:T(8,128)}, u32[]{:S(2)}) copy-start(s32[6,256]{1,0:T(8,128)} %param.11) | copy-start | bytes 18436
  126.1 11.4 %collective-permute-start.20 = (bf16[4,96,256]{2,1,0:T(8,128)(2,1)}, bf16[4,96,256]{2,1,0:T(8,128)(2,1)S(1)}, u32[]{:S(2)}, u32[]{:S(2)}) collective-permute-start(bf16[4,96,256]{2,1,0:T(8,128)(2,1)} %bitcast.31), channel_id=1, source_target_pairs={{0,128},{16,144},{32,160},{48,176},{64,192},{80,208},{96,224},{112... | collective-permute-start | bytes 589832 | tf_op jit(solution)/shard_map/ppermute | solution.py:228
  129.2 9.2 %collective-permute-start.21 = (bf16[4,96,256]{2,1,0:T(8,128)(2,1)}, bf16[4,96,256]{2,1,0:T(8,128)(2,1)S(1)}, u32[]{:S(2)}, u32[]{:S(2)}) collective-permute-start(bf16[4,96,256]{2,1,0:T(8,128)(2,1)} %bitcast.32), channel_id=1, source_target_pairs={{0,192},{16,208},{32,224},{48,240},{64,0},{80,16},{96,32},{112,48}... | collective-permute-start | bytes 589832 | tf_op jit(solution)/shard_map/ppermute | solution.py:228
  138.6 13.5 %collective-permute-start.22 = (bf16[96,256]{1,0:T(8,128)(2,1)S(1)}, bf16[96,256]{1,0:T(8,128)(2,1)S(1)}, u32[]{:S(2)}, u32[]{:S(2)}) collective-permute-start(bf16[96,256]{1,0:T(8,128)(2,1)S(1)} %get-tuple-element.23), channel_id=1, source_target_pairs={{0,16},{16,32},{32,48},{48,0},{64,80},{80,96},{96,112},{112,64},{1... | collective-permute-start | bytes 147464 | tf_op jit(solution)/shard_map/ppermute | solution.py:228
  147.9 5.3 %collective-permute-start.23 = (bf16[96,256]{1,0:T(8,128)(2,1)S(1)}, bf16[96,256]{1,0:T(8,128)(2,1)S(1)}, u32[]{:S(2)}, u32[]{:S(2)}) collective-permute-start(bf16[96,256]{1,0:T(8,128)(2,1)S(1)} %get-tuple-element.22), channel_id=1, source_target_pairs={{0,32},{16,48},{32,0},{48,16},{64,96},{80,112},{96,64},{112,80},{1... | collective-permute-start | bytes 147464 | tf_op jit(solution)/shard_map/ppermute | solution.py:228
  147.9 5.3 %collective-permute-start.24 = (bf16[96,256]{1,0:T(8,128)(2,1)S(1)}, bf16[96,256]{1,0:T(8,128)(2,1)S(1)}, u32[]{:S(2)}, u32[]{:S(2)}) collective-permute-start(bf16[96,256]{1,0:T(8,128)(2,1)S(1)} %get-tuple-element.21), channel_id=1, source_target_pairs={{0,48},{16,0},{32,16},{48,32},{64,112},{80,64},{96,80},{112,96},{1... | collective-permute-start | bytes 147464 | tf_op jit(solution)/shard_map/ppermute | solution.py:228
  150.5 2.7 %copy-start.4 = (bf16[6,256,128]{2,1,0:T(8,128)(2,1)S(1)}, bf16[6,256,128]{2,1,0:T(8,128)(2,1)}, u32[]{:S(2)}) copy-start(bf16[6,256,128]{2,1,0:T(8,128)(2,1)} %d_ref.1) | copy-start | bytes 1179652
  (1 other events, 1.0 us)
